TPU v7x, 256 devices: a whole 4x4x8 slice. The times are simulated.
256 devices in a mesh: rows: 16 (over y, z_lo), cols: 16 (over x, z_hi, core).
Axes of the slice: x: 4, y: 4, z: 8 (z_hi: 2, z_lo: 4; z = z_hi * 4 + z_lo), core: 2. Of those that a mesh axis runs over, the one named last changes fastest.
Arguments:
- activations: bfloat16 [256, 256, 384], P('rows', 'cols'), may hold values from -6 to 6
- grad_out: bfloat16 [256, 256, 384], P('rows', 'cols'), may hold values from -6 to 6
- kernels: float32 [2, 7, 7, 384], replicated, may hold values from -0.875 to 0.875
- norm_gains: float32 [2, 384], replicated, may hold values from 0.5 to 1.5
- norm_shifts: float32 [2, 384], replicated, may hold values from -3 to 3
- w_in: bfloat16 [2, 384, 1536], replicated, may hold values from -0.3125 to 0.3125
- b_in: float32 [2, 1536], replicated, may hold values from -3 to 3
- w_out: bfloat16 [2, 384, 1536], replicated, may hold values from -0.15625 to 0.15625
Outputs:
- grad_in: bfloat16 [256, 256, 384], P('rows', 'cols')
- grad_kernels: float32 [2, 7, 7, 384], replicated
- grad_gains: float32 [2, 384], replicated
- grad_shifts: float32 [2, 384], replicated
- grad_b_in: float32 [2, 1536], replicated
- grad_w_in: float32 [2, 384, 1536], P(None, None, ('rows', 'cols'))
- grad_w_out: float32 [2, 384, 1536], P(None, None, ('rows', 'cols'))
All inputs are finite; a program needn't handle non-finite values.
Results may differ from a plain program's by a relative error of at most 0.017.
Values may be sent and summed in bfloat16 or wider, within the bound.
A program may use at most 128 MiB of HBM per device.

v0:
```python
import math
import jax
import jax.numpy as jnp
from jax import lax
from jax.sharding import PartitionSpec as P

EPSILON = 1e-06
ROOT_HALF = 0.7071067811865476
INV_ROOT_TAU = 0.3989422804014327


def with_halo(block, sides, width):
    for axis, dim in sides:
        count = lax.axis_size(axis)
        forward = [(i, i + 1) for i in range(count - 1)]
        backward = [(target, source) for source, target in forward]
        low = lax.ppermute(
            lax.slice_in_dim(block, block.shape[dim] - width, None, axis=dim), axis, forward
        )
        high = lax.ppermute(lax.slice_in_dim(block, 0, width, axis=dim), axis, backward)
        block = jnp.concatenate([low, block, high], axis=dim)
    return block


def gelu_parts(pre_act):
    normal_cdf = 0.5 * (1.0 + lax.erf(pre_act * ROOT_HALF))
    density = jnp.exp(-0.5 * pre_act * pre_act) * INV_ROOT_TAU
    return (pre_act * normal_cdf, normal_cdf + pre_act * density)


def conv_from(padded, kernel, out_rows, out_cols):
    running = jnp.zeros((out_rows, out_cols, padded.shape[2]), jnp.float32)
    for row_off in range(7):
        for col_off in range(7):
            running = (
                running
                + kernel[row_off, col_off]
                * padded[row_off : row_off + out_rows, col_off : col_off + out_cols]
            )
    return running


def conv_back(padded_grad, kernel, out_rows, out_cols):
    running = jnp.zeros((out_rows, out_cols, padded_grad.shape[2]), jnp.float32)
    for row_off in range(7):
        for col_off in range(7):
            running = (
                running
                + kernel[row_off, col_off]
                * padded_grad[
                    6 - row_off : 6 - row_off + out_rows, 6 - col_off : 6 - col_off + out_cols
                ]
            )
    return running


def kernel_grad(grad_z, padded_in):
    out_rows, out_cols = (grad_z.shape[0], grad_z.shape[1])
    kernel_taps = []
    for row_off in range(7):
        for col_off in range(7):
            kernel_taps.append(
                jnp.sum(
                    grad_z * padded_in[row_off : row_off + out_rows, col_off : col_off + out_cols],
                    axis=(0, 1),
                )
            )
    return jnp.stack(kernel_taps).reshape(7, 7, grad_z.shape[2])


def norm_fwd(source, gain, shift):
    center = source - jnp.mean(source, axis=-1, keepdims=True)
    inv_std = lax.rsqrt(jnp.mean(center * center, axis=-1, keepdims=True) + EPSILON)
    norm_hat = center * inv_std
    return (norm_hat, inv_std, (norm_hat * gain + shift).astype(jnp.bfloat16))


def norm_back(grad_n, norm_hat, inv_std, gain):
    scaled = grad_n * gain
    return inv_std * (
        scaled
        - jnp.mean(scaled, axis=-1, keepdims=True)
        - norm_hat * jnp.mean(scaled * norm_hat, axis=-1, keepdims=True)
    )


def mlp_hidden(normed_flat, weight_in, bias_in):
    pre_act = jnp.dot(normed_flat, weight_in, preferred_element_type=jnp.float32) + bias_in
    activation, gelu_slope = gelu_parts(pre_act)
    return (activation.astype(jnp.bfloat16), gelu_slope)


def mlp_forward(normed_flat, weight_in, bias_in, weight_out):
    act_b, gelu_slope = mlp_hidden(normed_flat, weight_in, bias_in)
    mixed = lax.dot_general(
        act_b, weight_out, (((1,), (1,)), ((), ())), preferred_element_type=jnp.float32
    )
    return (act_b, gelu_slope, mixed)


def input_rim(source):
    return with_halo(source, (("rows", 0), ("cols", 1)), 3)


def layer_back(
    grad_b,
    normed_flat,
    act_b,
    gelu_slope,
    norm_hat,
    inv_std,
    kernel,
    gain,
    weight_in,
    weight_out,
    padded_in,
):
    tile_rows, tile_cols, channels = grad_b.shape
    grad_flat = grad_b.reshape(-1, channels)
    grad_wo = lax.dot_general(
        grad_flat, act_b, (((0,), (0,)), ((), ())), preferred_element_type=jnp.float32
    )
    grad_pre = jnp.dot(grad_flat, weight_out, preferred_element_type=jnp.float32) * gelu_slope
    grad_preb = grad_pre.astype(jnp.bfloat16)
    grad_wi = lax.dot_general(
        normed_flat, grad_preb, (((0,), (0,)), ((), ())), preferred_element_type=jnp.float32
    )
    grad_bias = jnp.sum(grad_pre, axis=0)
    grad_n = lax.dot_general(
        grad_preb, weight_in, (((1,), (1,)), ((), ())), preferred_element_type=jnp.float32
    ).reshape(grad_b.shape)
    grad_gain = jnp.sum(grad_n * norm_hat, axis=(0, 1))
    grad_shift = jnp.sum(grad_n, axis=(0, 1))
    grad_z = norm_back(grad_n, norm_hat, inv_std, gain).astype(jnp.bfloat16)
    padded_grad = with_halo(grad_z, (("rows", 0), ("cols", 1)), 3)
    kernel_taps = kernel_grad(grad_z.astype(jnp.float32), padded_in)
    spread = conv_back(padded_grad.astype(jnp.float32), kernel, tile_rows, tile_cols)
    return (spread, kernel_taps, grad_gain, grad_shift, grad_bias, grad_wi, grad_wo)


def shards(activations, grad_out, kernels, norm_gains, norm_shifts, w_in, b_in, w_out):
    tile_rows, tile_cols, channels = activations.shape
    grad_scale = 1.0 / math.sqrt(
        tile_rows * tile_cols * lax.axis_size("rows") * lax.axis_size("cols")
    )
    padded_in = input_rim(activations).astype(jnp.float32)
    conv_one = conv_from(padded_in, kernels[0], tile_rows, tile_cols)
    hat_one, inv_one, normed_grid = norm_fwd(conv_one, norm_gains[0], norm_shifts[0])
    normed_one = normed_grid.reshape(-1, channels)
    act_one, slope_one, mixed_one = mlp_forward(normed_one, w_in[0], b_in[0], w_out[0])
    middle = (activations.astype(jnp.float32) + mixed_one.reshape(activations.shape)).astype(
        jnp.bfloat16
    )
    padded_mid = input_rim(middle)
    padded_mid_wide = padded_mid.astype(jnp.float32)
    conv_two = conv_from(padded_mid_wide, kernels[1], tile_rows, tile_cols)
    hat_two, inv_two, normed_grid_two = norm_fwd(conv_two, norm_gains[1], norm_shifts[1])
    normed_two = normed_grid_two.reshape(-1, channels)
    act_two, slope_two = mlp_hidden(normed_two, w_in[1], b_in[1])
    back_two = layer_back(
        grad_out,
        normed_two,
        act_two,
        slope_two,
        hat_two,
        inv_two,
        kernels[1],
        norm_gains[1],
        w_in[1],
        w_out[1],
        padded_mid_wide,
    )
    grad_mid = (grad_out.astype(jnp.float32) + back_two[0]).astype(jnp.bfloat16)
    back_one = layer_back(
        grad_mid,
        normed_one,
        act_one,
        slope_one,
        hat_one,
        inv_one,
        kernels[0],
        norm_gains[0],
        w_in[0],
        w_out[0],
        padded_in,
    )
    grad_in = (grad_mid.astype(jnp.float32) + back_one[0]).astype(jnp.bfloat16)
    grad_kernels, grad_gains, grad_shifts, grad_b_in = lax.psum(
        (
            jnp.stack([back_one[1], back_two[1]]) * grad_scale,
            jnp.stack([back_one[2], back_two[2]]) * grad_scale,
            jnp.stack([back_one[3], back_two[3]]) * grad_scale,
            jnp.stack([back_one[4], back_two[4]]) * grad_scale,
        ),
        ("rows", "cols"),
    )
    stacked_in = jnp.stack([back_one[5], back_two[5]]) * grad_scale
    stacked_out = jnp.stack([back_one[6], back_two[6]]) * grad_scale
    grad_w_in, grad_w_out = (
        lax.psum_scatter(stacked_in, ("rows", "cols"), scatter_dimension=2, tiled=True),
        lax.psum_scatter(stacked_out, ("rows", "cols"), scatter_dimension=2, tiled=True),
    )
    return (grad_in, grad_kernels, grad_gains, grad_shifts, grad_b_in, grad_w_in, grad_w_out)


def solution(mesh):
    return jax.shard_map(
        shards,
        mesh=mesh,
        in_specs=(P("rows", "cols", None), P("rows", "cols", None), P(), P(), P(), P(), P(), P()),
        out_specs=(
            P("rows", "cols", None),
            P(),
            P(),
            P(),
            P(),
            P(None, None, ("rows", "cols")),
            P(None, None, ("rows", "cols")),
        ),
        check_vma=False,
    )
```

profile of v0, /device:TPU:8, one launch (start us, length us, event | category | flops | bytes accessed | tf_op | source)
XLA Modules:
  0.0 460.9 jit_solution(10851110256736545179)
XLA Ops:
  8.0 6.4 %collective-permute-start.1 = (bf16[3,16,384]{2,1,0:T(8,128)(2,1)S(1)}, bf16[3,16,384]{2,1,0:T(8,128)(2,1)S(1)}, u32[]{:S(2)}, u32[]{:S(2)}) collective-permute-start(bf16[3,16,384]{2,1,0:T(8,128)(2,1)S(1)} %get-tuple-element.268), channel_id=1, source_target_pairs={{16,0},{32,16},{48,32},{64,48},{80,64},{96,80},{112,96},{128,112},... | collective-permute-start | bytes 110600 | tf_op jit(solution)/shard_map/ppermute | solution.py:20
  14.5 1.9 collective-permute-start
  16.4 1.1 fusion.234
  20.3 2.7 collective-permute-done
  23.0 1.0 constant_dynamic-update-slice_fusion.1
  24.1 1.3 collective-permute-start.2
  25.4 1.3 collective-permute-start.3
  27.3 5.9 %collective-permute-done.3 = bf16[22,3,384]{2,1,0:T(4,128)(2,1)S(1)} collective-permute-done((bf16[22,3,384]{2,1,0:T(4,128)(2,1)S(1)}, bf16[22,3,384]{2,1,0:T(4,128)(2,1)S(1)}, u32[]{:S(2)}, u32[]{:S(2)}) %collective-permute-start.3) | collective-permute-done | bytes 50720 | tf_op jit(solution)/shard_map/ppermute | solution.py:20
  33.4 3.8 fusion.226
  38.6 1.8 multiply_convert_fusion.1
  41.6 1.9 collective-permute-start.4
  43.5 6.6 %collective-permute-start.5 = (bf16[3,16,384]{2,1,0:T(8,128)(2,1)S(1)}, bf16[3,16,384]{2,1,0:T(8,128)(2,1)S(1)}, u32[]{:S(2)}, u32[]{:S(2)}) collective-permute-start(bf16[3,16,384]{2,1,0:T(8,128)(2,1)S(1)} %get-tuple-element.267), channel_id=1, source_target_pairs={{16,0},{32,16},{48,32},{64,48},{80,64},{96,80},{112,96},{128,112},... | collective-permute-start | bytes 110600 | tf_op jit(solution)/shard_map/ppermute | solution.py:20
  50.5 1.3 collective-permute-done.5
  51.8 7.6 %collective-permute-start.6 = (bf16[22,3,384]{2,1,0:T(4,128)(2,1)S(1)}, bf16[22,3,384]{2,1,0:T(4,128)(2,1)S(1)}, u32[]{:S(2)}, u32[]{:S(2)}) collective-permute-start(bf16[22,3,384]{2,1,0:T(4,128)(2,1)S(1)} %get-tuple-element.258), channel_id=1, source_target_pairs={{0,1},{1,2},{2,3},{3,4},{4,5},{5,6},{6,7},{7,8},{8,9},{9,10},{10,1... | collective-permute-start | bytes 152072 | tf_op jit(solution)/shard_map/ppermute | solution.py:17
  59.5 1.3 collective-permute-start.7
  61.0 2.3 collective-permute-done.7
  63.4 3.6 fusion.225
  68.6 1.5 fusion.228
  70.1 1.2 multiply_reduce_fusion
  71.3 0.9 fusion.123
  73.6 1.9 collective-permute-start.8
  75.5 7.1 %collective-permute-start.9 = (bf16[3,16,384]{2,1,0:T(8,128)(2,1)S(1)}, bf16[3,16,384]{2,1,0:T(8,128)(2,1)S(1)}, u32[]{:S(2)}, u32[]{:S(2)}) collective-permute-start(bf16[3,16,384]{2,1,0:T(8,128)(2,1)S(1)} %get-tuple-element.265), channel_id=1, source_target_pairs={{16,0},{32,16},{48,32},{64,48},{80,64},{96,80},{112,96},{128,112},... | collective-permute-start | bytes 110600 | tf_op jit(solution)/shard_map/ppermute | solution.py:20
  82.6 2.0 convolution_bitcast_fusion
  85.4 9.1 %collective-permute-start.10 = (bf16[22,3,384]{2,1,0:T(4,128)(2,1)}, bf16[22,3,384]{2,1,0:T(4,128)(2,1)}, u32[]{:S(2)}, u32[]{:S(2)}) collective-permute-start(bf16[22,3,384]{2,1,0:T(4,128)(2,1)} %get-tuple-element.256), channel_id=1, source_target_pairs={{0,1},{1,2},{2,3},{3,4},{4,5},{5,6},{6,7},{7,8},{8,9},{9,10},{10,1... | collective-permute-start | bytes 152072 | tf_op jit(solution)/shard_map/ppermute | solution.py:17
  94.5 1.3 collective-permute-start.11
  112.5 4.3 stack.447
  116.8 1.1 maximum_convert_fusion.2
  118.0 3.9 fusion.177
  121.9 0.9 fusion.227
  123.7 1.9 multiply_reduce_fusion.1
  125.7 1.5 fusion.74
  128.9 1.9 convolution_bitcast_fusion.1
  130.8 1.9 convolution_bitcast_fusion.3
  133.5 5.0 %maximum_multiply_fusion.1 = f32[2,384,1536]{2,1,0:T(8,128)} fusion(f32[1,384,1536]{2,1,0:T(8,128)} %convolution_bitcast_fusion, f32[1,384,1536]{2,1,0:T(8,128)} %convolution_bitcast_fusion.1), kind=kLoop, calls=%fused_computation.99 | loop fusion | flops 2359296 | bytes 9437184 | tf_op jit(solution)/shard_map/mul | solution.py:198
  138.5 8.2 %copy.28 = f32[2,384,1536]{1,0,2:T(2,128)} copy(f32[2,384,1536]{2,1,0:T(8,128)} %maximum_multiply_fusion.1) | data formatting | bytes 9437184 | tf_op jit(solution)/shard_map/mul | solution.py:198
  146.6 4.5 maximum_multiply_fusion
  151.1 8.2 %copy.26 = f32[2,384,1536]{1,0,2:T(2,128)} copy(f32[2,384,1536]{2,1,0:T(8,128)} %maximum_multiply_fusion) | data formatting | bytes 9437184 | tf_op jit(solution)/shard_map/mul | solution.py:197
  162.7 2.0 collective-permute-start.12
  164.7 6.6 %collective-permute-start.13 = (bf16[3,16,384]{2,1,0:T(8,128)(2,1)S(1)}, bf16[3,16,384]{2,1,0:T(8,128)(2,1)S(1)}, u32[]{:S(2)}, u32[]{:S(2)}) collective-permute-start(bf16[3,16,384]{2,1,0:T(8,128)(2,1)S(1)} %get-tuple-element.263), channel_id=1, source_target_pairs={{16,0},{32,16},{48,32},{64,48},{80,64},{96,80},{112,96},{128,112},... | collective-permute-start | bytes 110600 | tf_op jit(solution)/shard_map/ppermute | solution.py:20
  172.0 1.0 collective-permute-done.13
  173.1 1.9 collective-permute-start.14
  175.0 1.3 collective-permute-start.15
  176.3 88.6 %all-reduce.2 = (f32[2,384]{1,0:T(2,128)}, f32[2,384]{1,0:T(2,128)}, f32[2,1536]{1,0:T(2,128)}) all-reduce(f32[2,384]{1,0:T(2,128)S(1)} %maximum_multiply_fusion.4, f32[2,384]{1,0:T(2,128)S(1)} %maximum_multiply_fusion.5, f32[2,1536]{1,0:T(2,128)S(1)} %maximum_multiply_fusion.3), channel_id=1, replica_groups=mesh['rows'=16,'cols'=16] {'rows','cols'}, use_global_device_ids=true, to_apply=%region_109.0 | all-reduce | flops 4608 | bytes 36864 | tf_op jit(solution)/shard_map/psum | solution.py:188
  265.4 4.2 fusion.127
  269.6 180.2 %all-reduce.6.cloned.1.call-done = (f32[2,7,7,384]{3,2,1,0:T(8,128)}, f32[2,384,1536]{1,0,2:T(2,128)}, f32[2,384,1536]{1,0,2:T(2,128)}) async-done(((f32[2,7,7,384]{3,2,1,0:T(8,128)}, f32[2,384,1536]{1,0,2:T(2,128)}, f32[2,384,1536]{1,0,2:T(2,128)}), (f32[2,7,7,384]{3,2,1,0:T(8,128)}, f32[2,384,1536]{1,0,2:T(2,128)}, f32[2,384,1536]{1,0,2:T(2,128)})) %all-reduce.6.cloned.1.call-update) | async-done | bytes 9587728 | tf_op jit(solution)/shard_map/psum | solution.py:188
  449.8 1.7 copy.29
  451.4 1.3 constant_dynamic-slice_fusion.1
  452.7 1.3 constant_dynamic-slice_fusion
  (417 shorter events, 34.1 us)
Async XLA Ops:
  7.2 442.6 %all-reduce.6.cloned.1.call-start = ((), (), s32[]{:S(2)}) async-start(), calls=%async_computation | async-start | bytes 19218432 | tf_op jit(solution)/shard_map/psum | solution.py:188
  8.0 15.9 %collective-permute-start.1 = (bf16[3,16,384]{2,1,0:T(8,128)(2,1)S(1)}, bf16[3,16,384]{2,1,0:T(8,128)(2,1)S(1)}, u32[]{:S(2)}, u32[]{:S(2)}) collective-permute-start(bf16[3,16,384]{2,1,0:T(8,128)(2,1)S(1)} %get-tuple-element.268), channel_id=1, source_target_pairs={{16,0},{32,16},{48,32},{64,48},{80,64},{96,80},{112,96},{128,112},... | collective-permute-start | bytes 110600 | tf_op jit(solution)/shard_map/ppermute | solution.py:20
  14.5 8.5 %collective-permute-start = (bf16[3,16,384]{2,1,0:T(8,128)(2,1)S(1)}, bf16[3,16,384]{2,1,0:T(8,128)(2,1)S(1)}, u32[]{:S(2)}, u32[]{:S(2)}) collective-permute-start(bf16[3,16,384]{2,1,0:T(8,128)(2,1)S(1)} %get-tuple-element.269), channel_id=1, source_target_pairs={{0,16},{16,32},{32,48},{48,64},{64,80},{80,96},{96,112},{112,128},... | collective-permute-start | bytes 110600 | tf_op jit(solution)/shard_map/ppermute | solution.py:17
  24.1 3.2 collective-permute-start.2
  25.4 7.9 %collective-permute-start.3 = (bf16[22,3,384]{2,1,0:T(4,128)(2,1)S(1)}, bf16[22,3,384]{2,1,0:T(4,128)(2,1)S(1)}, u32[]{:S(2)}, u32[]{:S(2)}) collective-permute-start(bf16[22,3,384]{2,1,0:T(4,128)(2,1)S(1)} %get-tuple-element.261), channel_id=1, source_target_pairs={{1,0},{2,1},{3,2},{4,3},{5,4},{6,5},{7,6},{8,7},{9,8},{10,9},{11,1... | collective-permute-start | bytes 152072 | tf_op jit(solution)/shard_map/ppermute | solution.py:20
  41.6 8.9 %collective-permute-start.4 = (bf16[3,16,384]{2,1,0:T(8,128)(2,1)S(1)}, bf16[3,16,384]{2,1,0:T(8,128)(2,1)S(1)}, u32[]{:S(2)}, u32[]{:S(2)}) collective-permute-start(bf16[3,16,384]{2,1,0:T(8,128)(2,1)S(1)} %get-tuple-element.266), channel_id=1, source_target_pairs={{0,16},{16,32},{32,48},{48,64},{64,80},{80,96},{96,112},{112,128},... | collective-permute-start | bytes 110600 | tf_op jit(solution)/shard_map/ppermute | solution.py:17
  43.5 8.2 %collective-permute-start.5 = (bf16[3,16,384]{2,1,0:T(8,128)(2,1)S(1)}, bf16[3,16,384]{2,1,0:T(8,128)(2,1)S(1)}, u32[]{:S(2)}, u32[]{:S(2)}) collective-permute-start(bf16[3,16,384]{2,1,0:T(8,128)(2,1)S(1)} %get-tuple-element.267), channel_id=1, source_target_pairs={{16,0},{32,16},{48,32},{64,48},{80,64},{96,80},{112,96},{128,112},... | collective-permute-start | bytes 110600 | tf_op jit(solution)/shard_map/ppermute | solution.py:20
  51.8 9.1 %collective-permute-start.6 = (bf16[22,3,384]{2,1,0:T(4,128)(2,1)S(1)}, bf16[22,3,384]{2,1,0:T(4,128)(2,1)S(1)}, u32[]{:S(2)}, u32[]{:S(2)}) collective-permute-start(bf16[22,3,384]{2,1,0:T(4,128)(2,1)S(1)} %get-tuple-element.258), channel_id=1, source_target_pairs={{0,1},{1,2},{2,3},{3,4},{4,5},{5,6},{6,7},{7,8},{8,9},{9,10},{10,1... | collective-permute-start | bytes 152072 | tf_op jit(solution)/shard_map/ppermute | solution.py:17
  59.5 3.8 collective-permute-start.7
  73.6 11.1 %collective-permute-start.8 = (bf16[3,16,384]{2,1,0:T(8,128)(2,1)S(1)}, bf16[3,16,384]{2,1,0:T(8,128)(2,1)S(1)}, u32[]{:S(2)}, u32[]{:S(2)}) collective-permute-start(bf16[3,16,384]{2,1,0:T(8,128)(2,1)S(1)} %get-tuple-element.264), channel_id=1, source_target_pairs={{0,16},{16,32},{32,48},{48,64},{64,80},{80,96},{96,112},{112,128},... | collective-permute-start | bytes 110600 | tf_op jit(solution)/shard_map/ppermute | solution.py:17
  75.5 9.1 %collective-permute-start.9 = (bf16[3,16,384]{2,1,0:T(8,128)(2,1)S(1)}, bf16[3,16,384]{2,1,0:T(8,128)(2,1)S(1)}, u32[]{:S(2)}, u32[]{:S(2)}) collective-permute-start(bf16[3,16,384]{2,1,0:T(8,128)(2,1)S(1)} %get-tuple-element.265), channel_id=1, source_target_pairs={{16,0},{32,16},{48,32},{64,48},{80,64},{96,80},{112,96},{128,112},... | collective-permute-start | bytes 110600 | tf_op jit(solution)/shard_map/ppermute | solution.py:20
  85.4 31.5 %collective-permute-start.10 = (bf16[22,3,384]{2,1,0:T(4,128)(2,1)}, bf16[22,3,384]{2,1,0:T(4,128)(2,1)}, u32[]{:S(2)}, u32[]{:S(2)}) collective-permute-start(bf16[22,3,384]{2,1,0:T(4,128)(2,1)} %get-tuple-element.256), channel_id=1, source_target_pairs={{0,1},{1,2},{2,3},{3,4},{4,5},{5,6},{6,7},{7,8},{8,9},{9,10},{10,1... | collective-permute-start | bytes 152072 | tf_op jit(solution)/shard_map/ppermute | solution.py:17
  94.5 22.4 %collective-permute-start.11 = (bf16[22,3,384]{2,1,0:T(4,128)(2,1)}, bf16[22,3,384]{2,1,0:T(4,128)(2,1)}, u32[]{:S(2)}, u32[]{:S(2)}) collective-permute-start(bf16[22,3,384]{2,1,0:T(4,128)(2,1)} %get-tuple-element.257), channel_id=1, source_target_pairs={{1,0},{2,1},{3,2},{4,3},{5,4},{6,5},{7,6},{8,7},{9,8},{10,9},{11,1... | collective-permute-start | bytes 152072 | tf_op jit(solution)/shard_map/ppermute | solution.py:20
  160.0 105.0 %copy-start.3 = (bf16[16,16,384]{2,1,0:T(8,128)(2,1)S(1)}, bf16[16,16,384]{2,1,0:T(8,128)(2,1)}, u32[]{:S(2)}) copy-start(bf16[16,16,384]{2,1,0:T(8,128)(2,1)} %copy-done.2) | copy-start | bytes 589828
  160.0 105.0 %copy-start.15 = (f32[384]{0:T(512)S(1)}, f32[384]{0:T(512)}, u32[]{:S(2)}) copy-start(f32[384]{0:T(512)} %copy-done.14) | copy-start | bytes 4612
  160.0 105.0 %copy-start.17 = (f32[384]{0:T(512)S(1)}, f32[384]{0:T(512)}, u32[]{:S(2)}) copy-start(f32[384]{0:T(512)} %copy-done.16) | copy-start | bytes 4612
  160.0 105.0 %copy-start.19 = (f32[384]{0:T(512)S(1)}, f32[384]{0:T(512)}, u32[]{:S(2)}) copy-start(f32[384]{0:T(512)} %copy-done.18) | copy-start | bytes 4612
  160.1 105.0 %copy-start.21 = (f32[384]{0:T(512)S(1)}, f32[384]{0:T(512)}, u32[]{:S(2)}) copy-start(f32[384]{0:T(512)} %copy-done.20) | copy-start | bytes 4612
  160.1 105.0 %copy-start.23 = (f32[384]{0:T(512)S(1)}, f32[384]{0:T(512)}, u32[]{:S(2)}) copy-start(f32[384]{0:T(512)} %copy-done.22) | copy-start | bytes 4612
  160.1 105.0 %copy-start.25 = (f32[384]{0:T(512)S(1)}, f32[384]{0:T(512)}, u32[]{:S(2)}) copy-start(f32[384]{0:T(512)} %copy-done.24) | copy-start | bytes 4612
  160.1 105.0 %copy-start.27 = (f32[384]{0:T(512)S(1)}, f32[384]{0:T(512)}, u32[]{:S(2)}) copy-start(f32[384]{0:T(512)} %copy-done.26) | copy-start | bytes 4612
  160.1 105.0 %copy-start.29 = (f32[384]{0:T(512)S(1)}, f32[384]{0:T(512)}, u32[]{:S(2)}) copy-start(f32[384]{0:T(512)} %copy-done.28) | copy-start | bytes 4612
  160.1 105.0 %copy-start.31 = (f32[384]{0:T(512)S(1)}, f32[384]{0:T(512)}, u32[]{:S(2)}) copy-start(f32[384]{0:T(512)} %copy-done.30) | copy-start | bytes 4612
  160.1 105.0 %copy-start.33 = (f32[384]{0:T(512)S(1)}, f32[384]{0:T(512)}, u32[]{:S(2)}) copy-start(f32[384]{0:T(512)} %copy-done.32) | copy-start | bytes 4612
  160.1 105.0 %copy-start.35 = (f32[384]{0:T(512)S(1)}, f32[384]{0:T(512)}, u32[]{:S(2)}) copy-start(f32[384]{0:T(512)} %copy-done.34) | copy-start | bytes 4612
  160.1 105.0 %copy-start.37 = (f32[384]{0:T(512)S(1)}, f32[384]{0:T(512)}, u32[]{:S(2)}) copy-start(f32[384]{0:T(512)} %copy-done.36) | copy-start | bytes 4612
  160.1 105.0 %copy-start.39 = (f32[384]{0:T(512)S(1)}, f32[384]{0:T(512)}, u32[]{:S(2)}) copy-start(f32[384]{0:T(512)} %copy-done.38) | copy-start | bytes 4612
  160.2 105.0 %copy-start.41 = (f32[384]{0:T(512)S(1)}, f32[384]{0:T(512)}, u32[]{:S(2)}) copy-start(f32[384]{0:T(512)} %copy-done.40) | copy-start | bytes 4612
  160.2 105.0 %copy-start.43 = (f32[384]{0:T(512)S(1)}, f32[384]{0:T(512)}, u32[]{:S(2)}) copy-start(f32[384]{0:T(512)} %copy-done.42) | copy-start | bytes 4612
  160.2 105.0 %copy-start.45 = (f32[384]{0:T(512)S(1)}, f32[384]{0:T(512)}, u32[]{:S(2)}) copy-start(f32[384]{0:T(512)} %copy-done.44) | copy-start | bytes 4612
  160.2 105.0 %copy-start.47 = (f32[384]{0:T(512)S(1)}, f32[384]{0:T(512)}, u32[]{:S(2)}) copy-start(f32[384]{0:T(512)} %copy-done.46) | copy-start | bytes 4612
  160.2 105.0 %copy-start.49 = (f32[384]{0:T(512)S(1)}, f32[384]{0:T(512)}, u32[]{:S(2)}) copy-start(f32[384]{0:T(512)} %copy-done.48) | copy-start | bytes 4612
  160.2 105.0 %copy-start.51 = (f32[384]{0:T(512)S(1)}, f32[384]{0:T(512)}, u32[]{:S(2)}) copy-start(f32[384]{0:T(512)} %copy-done.50) | copy-start | bytes 4612
  160.2 105.0 %copy-start.53 = (f32[384]{0:T(512)S(1)}, f32[384]{0:T(512)}, u32[]{:S(2)}) copy-start(f32[384]{0:T(512)} %copy-done.52) | copy-start | bytes 4612
  160.2 105.0 %copy-start.55 = (f32[384]{0:T(512)S(1)}, f32[384]{0:T(512)}, u32[]{:S(2)}) copy-start(f32[384]{0:T(512)} %copy-done.54) | copy-start | bytes 4612
  160.2 105.0 %copy-start.57 = (f32[384]{0:T(512)S(1)}, f32[384]{0:T(512)}, u32[]{:S(2)}) copy-start(f32[384]{0:T(512)} %copy-done.56) | copy-start | bytes 4612
  160.2 105.0 %copy-start.59 = (f32[384]{0:T(512)S(1)}, f32[384]{0:T(512)}, u32[]{:S(2)}) copy-start(f32[384]{0:T(512)} %copy-done.58) | copy-start | bytes 4612
  160.3 105.0 %copy-start.61 = (f32[384]{0:T(512)S(1)}, f32[384]{0:T(512)}, u32[]{:S(2)}) copy-start(f32[384]{0:T(512)} %copy-done.60) | copy-start | bytes 4612
  160.3 105.0 %copy-start.63 = (f32[384]{0:T(512)S(1)}, f32[384]{0:T(512)}, u32[]{:S(2)}) copy-start(f32[384]{0:T(512)} %copy-done.62) | copy-start | bytes 4612
  160.3 105.0 %copy-start.65 = (f32[384]{0:T(512)S(1)}, f32[384]{0:T(512)}, u32[]{:S(2)}) copy-start(f32[384]{0:T(512)} %copy-done.64) | copy-start | bytes 4612
  160.3 105.0 %copy-start.67 = (f32[384]{0:T(512)S(1)}, f32[384]{0:T(512)}, u32[]{:S(2)}) copy-start(f32[384]{0:T(512)} %copy-done.66) | copy-start | bytes 4612
  160.3 105.0 %copy-start.69 = (f32[384]{0:T(512)S(1)}, f32[384]{0:T(512)}, u32[]{:S(2)}) copy-start(f32[384]{0:T(512)} %copy-done.68) | copy-start | bytes 4612
  160.3 105.0 %copy-start.71 = (f32[384]{0:T(512)S(1)}, f32[384]{0:T(512)}, u32[]{:S(2)}) copy-start(f32[384]{0:T(512)} %copy-done.70) | copy-start | bytes 4612
  160.3 105.0 %copy-start.73 = (f32[384]{0:T(512)S(1)}, f32[384]{0:T(512)}, u32[]{:S(2)}) copy-start(f32[384]{0:T(512)} %copy-done.72) | copy-start | bytes 4612
  162.7 9.3 %collective-permute-start.12 = (bf16[3,16,384]{2,1,0:T(8,128)(2,1)S(1)}, bf16[3,16,384]{2,1,0:T(8,128)(2,1)S(1)}, u32[]{:S(2)}, u32[]{:S(2)}) collective-permute-start(bf16[3,16,384]{2,1,0:T(8,128)(2,1)S(1)} %get-tuple-element.262), channel_id=1, source_target_pairs={{0,16},{16,32},{32,48},{48,64},{64,80},{80,96},{96,112},{112,128},... | collective-permute-start | bytes 110600 | tf_op jit(solution)/shard_map/ppermute | solution.py:17
  164.7 8.3 %collective-permute-start.13 = (bf16[3,16,384]{2,1,0:T(8,128)(2,1)S(1)}, bf16[3,16,384]{2,1,0:T(8,128)(2,1)S(1)}, u32[]{:S(2)}, u32[]{:S(2)}) collective-permute-start(bf16[3,16,384]{2,1,0:T(8,128)(2,1)S(1)} %get-tuple-element.263), channel_id=1, source_target_pairs={{16,0},{32,16},{48,32},{64,48},{80,64},{96,80},{112,96},{128,112},... | collective-permute-start | bytes 110600 | tf_op jit(solution)/shard_map/ppermute | solution.py:20
  173.1 91.8 %collective-permute-start.14 = (bf16[22,3,384]{2,1,0:T(4,128)(2,1)S(1)}, bf16[22,3,384]{2,1,0:T(4,128)(2,1)S(1)}, u32[]{:S(2)}, u32[]{:S(2)}) collective-permute-start(bf16[22,3,384]{2,1,0:T(4,128)(2,1)S(1)} %get-tuple-element.254), channel_id=1, source_target_pairs={{0,1},{1,2},{2,3},{3,4},{4,5},{5,6},{6,7},{7,8},{8,9},{9,10},{10,1... | collective-permute-start | bytes 152072 | tf_op jit(solution)/shard_map/ppermute | solution.py:17
  175.0 89.9 %collective-permute-start.15 = (bf16[22,3,384]{2,1,0:T(4,128)(2,1)S(1)}, bf16[22,3,384]{2,1,0:T(4,128)(2,1)S(1)}, u32[]{:S(2)}, u32[]{:S(2)}) collective-permute-start(bf16[22,3,384]{2,1,0:T(4,128)(2,1)S(1)} %get-tuple-element.255), channel_id=1, source_target_pairs={{1,0},{2,1},{3,2},{4,3},{5,4},{6,5},{7,6},{8,7},{9,8},{10,9},{11,1... | collective-permute-start | bytes 152072 | tf_op jit(solution)/shard_map/ppermute | solution.py:20
  (95 other events, 2066.9 us)
Sparse Core Ops, SparseCore 0:
  160.1 289.5 all-reduce.5
where the time goes:
time: 463 us; the launch traced here: 461 us
  waiting for transfers between devices  193 us (42%)
  blocking collectives  88.6 us (19%)
  starting transfers between devices  59.6 us (13%)
  local copies, waits for them, and re-layouts  53.2 us (11%)
  other arithmetic  34.6 us (7%)
  between operations  16.7 us (4%)
  matrix products  14.8 us (3%)
    psum x1, waiting for transfers between devices, shards(): lax.psum((jnp.stack([back_one[1], back_two[1]]) * grad_scale, jnp.stack([...  180 us
    psum x1, blocking collectives, shards(): lax.psum((jnp.stack([back_one[1], back_two[1]]) * grad_scale, jnp.stack([...  88.6 us
    ppermute x8, starting transfers between devices, with_halo(): lax.ppermute(lax.slice_in_dim(block, 0, width, axis=dim), axis, backward)  31.9 us
    ppermute x8, starting transfers between devices, with_halo(): lax.ppermute(lax.slice_in_dim(block, block.shape[dim] - width, None, axis...  27.7 us
    another operation x100, local copies, waits for them, and re-layouts, kernel_grad(): return jnp.stack(kernel_taps).reshape(7, 7, grad_z.shape[2])  20.7 us
    ppermute x8, waiting for transfers between devices, with_halo(): lax.ppermute(lax.slice_in_dim(block, 0, width, axis=dim), axis, backward)  10.5 us
  transfers between devices with their start and end apart: 17, of which 6 were waited for; matrix products, arithmetic and copies ran while one was open for 8% of the time, Pallas kernels for 0%

commit v1 on v0

--- a/solution.py
+++ b/solution.py
@@ -186,13 +186,16 @@
     )
     grad_in = (grad_mid.astype(jnp.float32) + back_one[0]).astype(jnp.bfloat16)
     grad_kernels, grad_gains, grad_shifts, grad_b_in = lax.psum(
-        (
-            jnp.stack([back_one[1], back_two[1]]) * grad_scale,
-            jnp.stack([back_one[2], back_two[2]]) * grad_scale,
-            jnp.stack([back_one[3], back_two[3]]) * grad_scale,
-            jnp.stack([back_one[4], back_two[4]]) * grad_scale,
+        lax.psum(
+            (
+                jnp.stack([back_one[1], back_two[1]]) * grad_scale,
+                jnp.stack([back_one[2], back_two[2]]) * grad_scale,
+                jnp.stack([back_one[3], back_two[3]]) * grad_scale,
+                jnp.stack([back_one[4], back_two[4]]) * grad_scale,
+            ),
+            "cols",
         ),
-        ("rows", "cols"),
+        "rows",
     )
     stacked_in = jnp.stack([back_one[5], back_two[5]]) * grad_scale
     stacked_out = jnp.stack([back_one[6], back_two[6]]) * grad_scale

time: 463 us -> 756 us (1.63)
  waiting for transfers between devices: 193 us -> 425 us
  blocking collectives: 88.6 us -> 154 us
    unnamed x1 -> x4, waiting for transfers between devices: 0.02 us -> 238 us
    psum x0 -> x1, blocking collectives: none -> 69.2 us  [shards(): lax.psum(lax.psum((jnp.stack([back_one[1], back_two[1]]) * grad_scale, jn...]
    ppermute x8, waiting for transfers between devices: 2.76 us -> 15 us  [with_halo(): lax.ppermute(lax.slice_in_dim(block, block.shape[dim] - width, None, axis...]
    ppermute x8, starting transfers between devices: 31.9 us -> 20.9 us  [with_halo(): lax.ppermute(lax.slice_in_dim(block, 0, width, axis=dim), axis, backward)]
    ppermute x8, waiting for transfers between devices: 10.5 us -> 0.02 us  [with_halo(): lax.ppermute(lax.slice_in_dim(block, 0, width, axis=dim), axis, backward)]
    ppermute x8, starting transfers between devices: 27.7 us -> 36.2 us  [with_halo(): lax.ppermute(lax.slice_in_dim(block, block.shape[dim] - width, None, axis...]
  transfers between devices with their start and end apart: 17 -> 19, of which waited for: 6 -> 7; matrix products, arithmetic and copies ran while one was open for 8% -> 8% of each run, Pallas kernels for 0% -> 0%
where the time goes in v1:
time: 756 us; the launch traced here: 754 us
  waiting for transfers between devices  425 us (56%)
  blocking collectives  154 us (20%)
  starting transfers between devices  57.3 us (8%)
  local copies, waits for them, and re-layouts  52.3 us (7%)
  other arithmetic  34.3 us (5%)
  between operations  16.5 us (2%)
  matrix products  13.4 us (2%)
    unnamed x4, waiting for transfers between devices  238 us
    psum x1, waiting for transfers between devices, shards(): lax.psum((jnp.stack([back_one[1], back_two[1]]) * grad_scale, jnp.stack([...  173 us
    psum x1, blocking collectives, shards(): lax.psum((jnp.stack([back_one[1], back_two[1]]) * grad_scale, jnp.stack([...  85.2 us
    psum x1, blocking collectives, shards(): lax.psum(lax.psum((jnp.stack([back_one[1], back_two[1]]) * grad_scale, jn...  69.2 us
    ppermute x8, starting transfers between devices, with_halo(): lax.ppermute(lax.slice_in_dim(block, block.shape[dim] - width, None, axis...  36.2 us
    ppermute x8, starting transfers between devices, with_halo(): lax.ppermute(lax.slice_in_dim(block, 0, width, axis=dim), axis, backward)  20.9 us
    another operation x100, local copies, waits for them, and re-layouts, kernel_grad(): return jnp.stack(kernel_taps).reshape(7, 7, grad_z.shape[2])  20.3 us
  transfers between devices with their start and end apart: 19, of which 7 were waited for; matrix products, arithmetic and copies ran while one was open for 8% of the time, Pallas kernels for 0%

profile of v1, /device:TPU:8, one launch (start us, length us, event | category | flops | bytes accessed | tf_op | source)
XLA Modules:
  0.0 753.6 jit_solution(15610306557100083586)
XLA Ops:
  8.0 3.8 collective-permute-start
  11.9 4.7 collective-permute-start.1
  16.6 1.1 fusion.234
  20.5 1.0 constant_dynamic-update-slice_fusion.1
  21.6 1.3 collective-permute-start.3
  22.9 3.0 collective-permute-start.2
  27.0 3.8 fusion.226
  32.2 1.8 multiply_convert_fusion.1
  35.2 3.7 collective-permute-start.5
  38.9 2.1 collective-permute-start.4
  41.3 6.3 collective-permute-done.4
  47.7 1.3 collective-permute-start.7
  49.0 8.0 %collective-permute-start.6 = (bf16[22,3,384]{2,1,0:T(4,128)(2,1)S(1)}, bf16[22,3,384]{2,1,0:T(4,128)(2,1)S(1)}, u32[]{:S(2)}, u32[]{:S(2)}) collective-permute-start(bf16[22,3,384]{2,1,0:T(4,128)(2,1)S(1)} %get-tuple-element.260), channel_id=1, source_target_pairs={{0,1},{1,2},{2,3},{3,4},{4,5},{5,6},{6,7},{7,8},{8,9},{9,10},{10,1... | collective-permute-start | bytes 152072 | tf_op jit(solution)/shard_map/ppermute | solution.py:17
  58.1 3.6 fusion.225
  63.3 1.5 fusion.228
  64.8 1.2 multiply_reduce_fusion
  66.0 0.9 fusion.123
  68.3 1.9 collective-permute-start.9
  70.2 4.1 collective-permute-start.8
  74.3 2.0 convolution_bitcast_fusion
  76.3 2.4 collective-permute-done.8
  79.5 1.3 collective-permute-start.11
  80.8 10.2 %collective-permute-start.10 = (bf16[22,3,384]{2,1,0:T(4,128)(2,1)}, bf16[22,3,384]{2,1,0:T(4,128)(2,1)}, u32[]{:S(2)}, u32[]{:S(2)}) collective-permute-start(bf16[22,3,384]{2,1,0:T(4,128)(2,1)} %get-tuple-element.258), channel_id=1, source_target_pairs={{0,1},{1,2},{2,3},{3,4},{4,5},{5,6},{6,7},{7,8},{8,9},{9,10},{10,1... | collective-permute-start | bytes 152072 | tf_op jit(solution)/shard_map/ppermute | solution.py:17
  107.9 3.6 stack.447
  111.6 1.1 maximum_convert_fusion.2
  112.7 3.9 fusion.177
  116.7 0.9 fusion.227
  118.5 1.9 multiply_reduce_fusion.1
  120.5 1.5 fusion.74
  122.6 0.8 fusion.75
  123.5 1.9 convolution_bitcast_fusion.3
  126.9 4.5 maximum_multiply_fusion
  131.9 172.8 %all-reduce.9.cloned.1.call-done = f32[2,7,7,384]{3,2,1,0:T(8,128)} async-done(((f32[2,7,7,384]{3,2,1,0:T(8,128)}), f32[2,7,7,384]{3,2,1,0:T(8,128)}) %all-reduce.9.cloned.1.call-update) | async-done | bytes 150544 | tf_op jit(solution)/shard_map/psum | solution.py:189
  304.8 4.7 maximum_multiply_fusion.1
  309.6 8.2 %copy.26 = f32[2,384,1536]{1,0,2:T(2,128)} copy(f32[2,384,1536]{2,1,0:T(8,128)} %maximum_multiply_fusion) | data formatting | bytes 9437184 | tf_op jit(solution)/shard_map/mul | solution.py:200
  317.7 8.2 %copy.28 = f32[2,384,1536]{1,0,2:T(2,128)} copy(f32[2,384,1536]{2,1,0:T(8,128)} %maximum_multiply_fusion.1) | data formatting | bytes 9437184 | tf_op jit(solution)/shard_map/mul | solution.py:201
  327.7 5.4 collective-permute-start.13
  333.1 1.9 collective-permute-start.12
  336.5 5.2 collective-permute-done.12
  341.8 1.3 collective-permute-start.15
  343.1 3.0 collective-permute-start.14
  346.1 85.2 %all-reduce.3 = (f32[2,384]{1,0:T(2,128)S(1)}, f32[2,384]{1,0:T(2,128)S(1)}, f32[2,1536]{1,0:T(2,128)S(1)}) all-reduce(f32[2,384]{1,0:T(2,128)S(1)} %maximum_multiply_fusion.4, f32[2,384]{1,0:T(2,128)S(1)} %maximum_multiply_fusion.5, f32[2,1536]{1,0:T(2,128)S(1)} %maximum_multiply_fusion.3), channel_id=1, replica_groups=mesh['rows'=16,'cols'=16] {'cols'}, use_global_device_ids=true, to_apply=%region_110.0 | all-reduce | flops 4608 | bytes 36864 | tf_op jit(solution)/shard_map/psum | solution.py:189
  431.4 69.2 %all-reduce.4 = (f32[2,384]{1,0:T(2,128)}, f32[2,384]{1,0:T(2,128)}, f32[2,1536]{1,0:T(2,128)}) all-reduce(f32[2,384]{1,0:T(2,128)S(1)} %get-tuple-element.240, f32[2,384]{1,0:T(2,128)S(1)} %get-tuple-element.241, f32[2,1536]{1,0:T(2,128)S(1)} %get-tuple-element.242), channel_id=1, replica_groups=mesh['rows'=16,'cols'=16] {'rows'}, use_global_device_ids=true, to_apply=%region_111.0 | all-reduce | flops 4608 | bytes 36864 | tf_op jit(solution)/shard_map/psum | solution.py:188
  501.2 4.1 fusion.127
  505.3 1.7 copy.29
  506.9 237.5 %all-reduce.13.cloned.1.call-done = (f32[2,384,1536]{1,0,2:T(2,128)}, f32[2,384,1536]{1,0,2:T(2,128)}) async-done(((f32[2,384,1536]{1,0,2:T(2,128)}, f32[2,384,1536]{1,0,2:T(2,128)}), (f32[2,384,1536]{1,0,2:T(2,128)}, f32[2,384,1536]{1,0,2:T(2,128)})) %all-reduce.13.cloned.1.call-update) | async-done | bytes 9437200
  744.4 1.3 constant_dynamic-slice_fusion.1
  745.8 1.3 constant_dynamic-slice_fusion
  (426 shorter events, 34.6 us)
Async XLA Ops:
  7.2 297.6 %all-reduce.9.cloned.1.call-start = ((), (), s32[]{:S(2)}) async-start(), calls=%async_computation | async-start | bytes 344064 | tf_op jit(solution)/shard_map/psum | solution.py:189
  8.0 12.5 %collective-permute-start = (bf16[3,16,384]{2,1,0:T(8,128)(2,1)S(1)}, bf16[3,16,384]{2,1,0:T(8,128)(2,1)S(1)}, u32[]{:S(2)}, u32[]{:S(2)}) collective-permute-start(bf16[3,16,384]{2,1,0:T(8,128)(2,1)S(1)} %get-tuple-element.271), channel_id=1, source_target_pairs={{0,16},{16,32},{32,48},{48,64},{64,80},{80,96},{96,112},{112,128},... | collective-permute-start | bytes 110600 | tf_op jit(solution)/shard_map/ppermute | solution.py:17
  11.9 9.6 %collective-permute-start.1 = (bf16[3,16,384]{2,1,0:T(8,128)(2,1)S(1)}, bf16[3,16,384]{2,1,0:T(8,128)(2,1)S(1)}, u32[]{:S(2)}, u32[]{:S(2)}) collective-permute-start(bf16[3,16,384]{2,1,0:T(8,128)(2,1)S(1)} %get-tuple-element.270), channel_id=1, source_target_pairs={{16,0},{32,16},{48,32},{64,48},{80,64},{96,80},{112,96},{128,112},... | collective-permute-start | bytes 110600 | tf_op jit(solution)/shard_map/ppermute | solution.py:20
  21.6 5.0 collective-permute-start.3
  22.9 3.9 collective-permute-start.2
  35.2 6.2 collective-permute-start.5
  38.9 8.8 %collective-permute-start.4 = (bf16[3,16,384]{2,1,0:T(8,128)(2,1)S(1)}, bf16[3,16,384]{2,1,0:T(8,128)(2,1)S(1)}, u32[]{:S(2)}, u32[]{:S(2)}) collective-permute-start(bf16[3,16,384]{2,1,0:T(8,128)(2,1)S(1)} %get-tuple-element.268), channel_id=1, source_target_pairs={{0,16},{16,32},{32,48},{48,64},{64,80},{80,96},{96,112},{112,128},... | collective-permute-start | bytes 110600 | tf_op jit(solution)/shard_map/ppermute | solution.py:17
  47.7 9.5 %collective-permute-start.7 = (bf16[22,3,384]{2,1,0:T(4,128)(2,1)S(1)}, bf16[22,3,384]{2,1,0:T(4,128)(2,1)S(1)}, u32[]{:S(2)}, u32[]{:S(2)}) collective-permute-start(bf16[22,3,384]{2,1,0:T(4,128)(2,1)S(1)} %get-tuple-element.261), channel_id=1, source_target_pairs={{1,0},{2,1},{3,2},{4,3},{5,4},{6,5},{7,6},{8,7},{9,8},{10,9},{11,1... | collective-permute-start | bytes 152072 | tf_op jit(solution)/shard_map/ppermute | solution.py:20
  49.0 8.9 %collective-permute-start.6 = (bf16[22,3,384]{2,1,0:T(4,128)(2,1)S(1)}, bf16[22,3,384]{2,1,0:T(4,128)(2,1)S(1)}, u32[]{:S(2)}, u32[]{:S(2)}) collective-permute-start(bf16[22,3,384]{2,1,0:T(4,128)(2,1)S(1)} %get-tuple-element.260), channel_id=1, source_target_pairs={{0,1},{1,2},{2,3},{3,4},{4,5},{5,6},{6,7},{7,8},{8,9},{9,10},{10,1... | collective-permute-start | bytes 152072 | tf_op jit(solution)/shard_map/ppermute | solution.py:17
  68.3 8.0 %collective-permute-start.9 = (bf16[3,16,384]{2,1,0:T(8,128)(2,1)S(1)}, bf16[3,16,384]{2,1,0:T(8,128)(2,1)S(1)}, u32[]{:S(2)}, u32[]{:S(2)}) collective-permute-start(bf16[3,16,384]{2,1,0:T(8,128)(2,1)S(1)} %get-tuple-element.267), channel_id=1, source_target_pairs={{16,0},{32,16},{48,32},{64,48},{80,64},{96,80},{112,96},{128,112},... | collective-permute-start | bytes 110600 | tf_op jit(solution)/shard_map/ppermute | solution.py:20
  70.2 8.5 %collective-permute-start.8 = (bf16[3,16,384]{2,1,0:T(8,128)(2,1)S(1)}, bf16[3,16,384]{2,1,0:T(8,128)(2,1)S(1)}, u32[]{:S(2)}, u32[]{:S(2)}) collective-permute-start(bf16[3,16,384]{2,1,0:T(8,128)(2,1)S(1)} %get-tuple-element.266), channel_id=1, source_target_pairs={{0,16},{16,32},{32,48},{48,64},{64,80},{80,96},{96,112},{112,128},... | collective-permute-start | bytes 110600 | tf_op jit(solution)/shard_map/ppermute | solution.py:17
  79.5 32.1 %collective-permute-start.11 = (bf16[22,3,384]{2,1,0:T(4,128)(2,1)}, bf16[22,3,384]{2,1,0:T(4,128)(2,1)}, u32[]{:S(2)}, u32[]{:S(2)}) collective-permute-start(bf16[22,3,384]{2,1,0:T(4,128)(2,1)} %get-tuple-element.259), channel_id=1, source_target_pairs={{1,0},{2,1},{3,2},{4,3},{5,4},{6,5},{7,6},{8,7},{9,8},{10,9},{11,1... | collective-permute-start | bytes 152072 | tf_op jit(solution)/shard_map/ppermute | solution.py:20
  80.8 30.8 %collective-permute-start.10 = (bf16[22,3,384]{2,1,0:T(4,128)(2,1)}, bf16[22,3,384]{2,1,0:T(4,128)(2,1)}, u32[]{:S(2)}, u32[]{:S(2)}) collective-permute-start(bf16[22,3,384]{2,1,0:T(4,128)(2,1)} %get-tuple-element.258), channel_id=1, source_target_pairs={{0,1},{1,2},{2,3},{3,4},{4,5},{5,6},{6,7},{7,8},{8,9},{9,10},{10,1... | collective-permute-start | bytes 152072 | tf_op jit(solution)/shard_map/ppermute | solution.py:17
  126.8 378.4 %all-reduce.11.cloned.1.call-start = ((), (), s32[]{:S(2)}) async-start(), calls=%async_computation.1 | async-start | bytes 344064 | tf_op jit(solution)/shard_map/psum | solution.py:188
  304.8 439.7 %all-reduce.13.cloned.1.call-start = ((), (), s32[]{:S(2)}) async-start(), calls=%async_computation.2 | async-start | bytes 18874368
  325.9 174.9 %copy-start.4 = (bf16[16,16,384]{2,1,0:T(8,128)(2,1)S(1)}, bf16[16,16,384]{2,1,0:T(8,128)(2,1)}, u32[]{:S(2)}) copy-start(bf16[16,16,384]{2,1,0:T(8,128)(2,1)} %copy-done.2) | copy-start | bytes 589828
  325.9 174.9 %copy-start.16 = (f32[384]{0:T(512)S(1)}, f32[384]{0:T(512)}, u32[]{:S(2)}) copy-start(f32[384]{0:T(512)} %copy-done.15) | copy-start | bytes 4612
  325.9 174.9 %copy-start.18 = (f32[384]{0:T(512)S(1)}, f32[384]{0:T(512)}, u32[]{:S(2)}) copy-start(f32[384]{0:T(512)} %copy-done.17) | copy-start | bytes 4612
  325.9 174.9 %copy-start.20 = (f32[384]{0:T(512)S(1)}, f32[384]{0:T(512)}, u32[]{:S(2)}) copy-start(f32[384]{0:T(512)} %copy-done.19) | copy-start | bytes 4612
  326.0 174.9 %copy-start.22 = (f32[384]{0:T(512)S(1)}, f32[384]{0:T(512)}, u32[]{:S(2)}) copy-start(f32[384]{0:T(512)} %copy-done.21) | copy-start | bytes 4612
  326.0 174.9 %copy-start.24 = (f32[384]{0:T(512)S(1)}, f32[384]{0:T(512)}, u32[]{:S(2)}) copy-start(f32[384]{0:T(512)} %copy-done.23) | copy-start | bytes 4612
  326.0 174.9 %copy-start.26 = (f32[384]{0:T(512)S(1)}, f32[384]{0:T(512)}, u32[]{:S(2)}) copy-start(f32[384]{0:T(512)} %copy-done.25) | copy-start | bytes 4612
  326.0 174.9 %copy-start.28 = (f32[384]{0:T(512)S(1)}, f32[384]{0:T(512)}, u32[]{:S(2)}) copy-start(f32[384]{0:T(512)} %copy-done.27) | copy-start | bytes 4612
  326.0 174.9 %copy-start.30 = (f32[384]{0:T(512)S(1)}, f32[384]{0:T(512)}, u32[]{:S(2)}) copy-start(f32[384]{0:T(512)} %copy-done.29) | copy-start | bytes 4612
  326.0 174.9 %copy-start.32 = (f32[384]{0:T(512)S(1)}, f32[384]{0:T(512)}, u32[]{:S(2)}) copy-start(f32[384]{0:T(512)} %copy-done.31) | copy-start | bytes 4612
  326.0 174.9 %copy-start.34 = (f32[384]{0:T(512)S(1)}, f32[384]{0:T(512)}, u32[]{:S(2)}) copy-start(f32[384]{0:T(512)} %copy-done.33) | copy-start | bytes 4612
  326.0 174.9 %copy-start.36 = (f32[384]{0:T(512)S(1)}, f32[384]{0:T(512)}, u32[]{:S(2)}) copy-start(f32[384]{0:T(512)} %copy-done.35) | copy-start | bytes 4612
  326.0 174.9 %copy-start.38 = (f32[384]{0:T(512)S(1)}, f32[384]{0:T(512)}, u32[]{:S(2)}) copy-start(f32[384]{0:T(512)} %copy-done.37) | copy-start | bytes 4612
  326.0 174.9 %copy-start.40 = (f32[384]{0:T(512)S(1)}, f32[384]{0:T(512)}, u32[]{:S(2)}) copy-start(f32[384]{0:T(512)} %copy-done.39) | copy-start | bytes 4612
  326.1 174.9 %copy-start.42 = (f32[384]{0:T(512)S(1)}, f32[384]{0:T(512)}, u32[]{:S(2)}) copy-start(f32[384]{0:T(512)} %copy-done.41) | copy-start | bytes 4612
  326.1 174.9 %copy-start.44 = (f32[384]{0:T(512)S(1)}, f32[384]{0:T(512)}, u32[]{:S(2)}) copy-start(f32[384]{0:T(512)} %copy-done.43) | copy-start | bytes 4612
  326.1 174.9 %copy-start.46 = (f32[384]{0:T(512)S(1)}, f32[384]{0:T(512)}, u32[]{:S(2)}) copy-start(f32[384]{0:T(512)} %copy-done.45) | copy-start | bytes 4612
  326.1 174.9 %copy-start.48 = (f32[384]{0:T(512)S(1)}, f32[384]{0:T(512)}, u32[]{:S(2)}) copy-start(f32[384]{0:T(512)} %copy-done.47) | copy-start | bytes 4612
  326.1 174.9 %copy-start.50 = (f32[384]{0:T(512)S(1)}, f32[384]{0:T(512)}, u32[]{:S(2)}) copy-start(f32[384]{0:T(512)} %copy-done.49) | copy-start | bytes 4612
  326.1 174.9 %copy-start.52 = (f32[384]{0:T(512)S(1)}, f32[384]{0:T(512)}, u32[]{:S(2)}) copy-start(f32[384]{0:T(512)} %copy-done.51) | copy-start | bytes 4612
  326.1 174.9 %copy-start.54 = (f32[384]{0:T(512)S(1)}, f32[384]{0:T(512)}, u32[]{:S(2)}) copy-start(f32[384]{0:T(512)} %copy-done.53) | copy-start | bytes 4612
  326.1 174.9 %copy-start.56 = (f32[384]{0:T(512)S(1)}, f32[384]{0:T(512)}, u32[]{:S(2)}) copy-start(f32[384]{0:T(512)} %copy-done.55) | copy-start | bytes 4612
  326.1 174.9 %copy-start.58 = (f32[384]{0:T(512)S(1)}, f32[384]{0:T(512)}, u32[]{:S(2)}) copy-start(f32[384]{0:T(512)} %copy-done.57) | copy-start | bytes 4612
  326.1 174.9 %copy-start.60 = (f32[384]{0:T(512)S(1)}, f32[384]{0:T(512)}, u32[]{:S(2)}) copy-start(f32[384]{0:T(512)} %copy-done.59) | copy-start | bytes 4612
  326.2 174.9 %copy-start.62 = (f32[384]{0:T(512)S(1)}, f32[384]{0:T(512)}, u32[]{:S(2)}) copy-start(f32[384]{0:T(512)} %copy-done.61) | copy-start | bytes 4612
  326.2 174.9 %copy-start.64 = (f32[384]{0:T(512)S(1)}, f32[384]{0:T(512)}, u32[]{:S(2)}) copy-start(f32[384]{0:T(512)} %copy-done.63) | copy-start | bytes 4612
  326.2 174.9 %copy-start.66 = (f32[384]{0:T(512)S(1)}, f32[384]{0:T(512)}, u32[]{:S(2)}) copy-start(f32[384]{0:T(512)} %copy-done.65) | copy-start | bytes 4612
  326.2 174.9 %copy-start.68 = (f32[384]{0:T(512)S(1)}, f32[384]{0:T(512)}, u32[]{:S(2)}) copy-start(f32[384]{0:T(512)} %copy-done.67) | copy-start | bytes 4612
  326.2 174.9 %copy-start.70 = (f32[384]{0:T(512)S(1)}, f32[384]{0:T(512)}, u32[]{:S(2)}) copy-start(f32[384]{0:T(512)} %copy-done.69) | copy-start | bytes 4612
  327.7 8.8 %collective-permute-start.13 = (bf16[3,16,384]{2,1,0:T(8,128)(2,1)S(1)}, bf16[3,16,384]{2,1,0:T(8,128)(2,1)S(1)}, u32[]{:S(2)}, u32[]{:S(2)}) collective-permute-start(bf16[3,16,384]{2,1,0:T(8,128)(2,1)S(1)} %get-tuple-element.265), channel_id=1, source_target_pairs={{16,0},{32,16},{48,32},{64,48},{80,64},{96,80},{112,96},{128,112},... | collective-permute-start | bytes 110600 | tf_op jit(solution)/shard_map/ppermute | solution.py:20
  333.1 8.6 %collective-permute-start.12 = (bf16[3,16,384]{2,1,0:T(8,128)(2,1)S(1)}, bf16[3,16,384]{2,1,0:T(8,128)(2,1)S(1)}, u32[]{:S(2)}, u32[]{:S(2)}) collective-permute-start(bf16[3,16,384]{2,1,0:T(8,128)(2,1)S(1)} %get-tuple-element.264), channel_id=1, source_target_pairs={{0,16},{16,32},{32,48},{48,64},{64,80},{80,96},{96,112},{112,128},... | collective-permute-start | bytes 110600 | tf_op jit(solution)/shard_map/ppermute | solution.py:17
  341.8 158.8 %collective-permute-start.15 = (bf16[22,3,384]{2,1,0:T(4,128)(2,1)S(1)}, bf16[22,3,384]{2,1,0:T(4,128)(2,1)S(1)}, u32[]{:S(2)}, u32[]{:S(2)}) collective-permute-start(bf16[22,3,384]{2,1,0:T(4,128)(2,1)S(1)} %get-tuple-element.257), channel_id=1, source_target_pairs={{1,0},{2,1},{3,2},{4,3},{5,4},{6,5},{7,6},{8,7},{9,8},{10,9},{11,1... | collective-permute-start | bytes 152072 | tf_op jit(solution)/shard_map/ppermute | solution.py:20
  343.1 157.5 %collective-permute-start.14 = (bf16[22,3,384]{2,1,0:T(4,128)(2,1)S(1)}, bf16[22,3,384]{2,1,0:T(4,128)(2,1)S(1)}, u32[]{:S(2)}, u32[]{:S(2)}) collective-permute-start(bf16[22,3,384]{2,1,0:T(4,128)(2,1)S(1)} %get-tuple-element.256), channel_id=1, source_target_pairs={{0,1},{1,2},{2,3},{3,4},{4,5},{5,6},{6,7},{7,8},{8,9},{9,10},{10,1... | collective-permute-start | bytes 152072 | tf_op jit(solution)/shard_map/ppermute | solution.py:17
  (98 other events, 2767.8 us)
Sparse Core Ops, SparseCore 0:
  127.0 177.7 all-reduce.8
  307.4 152.3 all-reduce.10
  465.5 278.8 all-reduce.12
